TPU v7x, 32 devices: a whole 2x2x4 slice. The times are simulated.
32 devices in a mesh: grp: 8 (over z, x), dev: 4 (over y, core).
Axes of the slice: x: 2, y: 2, z: 4, core: 2. Of those that a mesh axis runs over, the one named last changes fastest.
Arguments:
- node_src: bfloat16 [4096, 1024], P(('grp', 'dev'))
- hub_feat: bfloat16 [4096, 1024], P(('grp', 'dev'))
- w_query: bfloat16 [1024, 1024], replicated, may hold values from -0.1875 to 0.1875
- w_key: bfloat16 [1024, 1024], replicated, may hold values from -0.1875 to 0.1875
- w_value: bfloat16 [1024, 1024], replicated, may hold values from -0.1875 to 0.1875
- w_out: bfloat16 [1024, 1024], replicated, may hold values from -0.75 to 0.75
- w_att: bfloat16 [16, 16, 64, 64], replicated, may hold values from -0.75 to 0.75
- w_msg: bfloat16 [16, 16, 64, 64], replicated, may hold values from -0.75 to 0.75
- relation_prior: float32 [16, 16], replicated, may hold values from 0.5 to 2
- block_src: int32 [32, 40], P(('grp', 'dev')), may hold values from 0 to 7
- block_dst: int32 [32, 40], P(('grp', 'dev')), may hold values from 0 to 3
- block_type: int32 [32, 40], P(('grp', 'dev')), may hold values from 0 to 15
- block_count: int32 [32], P(('grp', 'dev')), may hold values from 20 to 40, as said below
Outputs:
- hub_out: bfloat16 [4096, 1024], P(('grp', 'dev'))
Inputs may be any that keep to these rules, and one draw needn't show every extreme that they name: `block_count`: some device uses all 40 slots; every hub tile of a group is the target of some used block of that group.
All inputs are finite; a program needn't handle non-finite values.
Results may differ from a plain program's by a relative error of at most 0.018.
The roundings to bfloat16 on the way count: a program that leaves them out, or rounds other values in their place, can miss the bound.
Values may be sent and summed in bfloat16 or wider, within the bound.
No kernel may reach another device: no remote copies, remote signals or barrier semaphores. Data moves between devices by JAX's collectives and lax.ppermute only.
A program may use at most 128 MiB of HBM per device.

v0:
```python
import jax
import jax.numpy as jnp
from jax import lax
from jax.sharding import PartitionSpec as P


def body(
    node_src,
    hub_feat,
    w_query,
    w_key,
    w_value,
    w_out,
    w_att,
    w_msg,
    relation_prior,
    block_src,
    block_dst,
    block_type,
    block_count,
):
    owners = lax.axis_size("dev")
    tile_rows = hub_feat.shape[0]
    width = hub_feat.shape[1]
    heads = relation_prior.shape[1]
    head_dim = width // heads
    group_hubs = owners * tile_rows
    queries = jnp.dot(hub_feat, w_query, preferred_element_type=jnp.float32).astype(jnp.bfloat16)
    all_queries = lax.all_gather(queries, "dev", axis=0, tiled=True)
    w_both = jnp.concatenate([w_key, w_value], axis=1)
    own_kv = jnp.dot(node_src, w_both, preferred_element_type=jnp.float32).astype(jnp.bfloat16)
    keyval = lax.all_gather(own_kv, "grp", axis=0, tiled=True)
    scale_root = jnp.sqrt(jnp.float32(head_dim))

    def one_block(slot, carry):
        highest, denom, total = carry
        src_tile = block_src[0, slot]
        dst_tile = block_dst[0, slot]
        rtype = block_type[0, slot]
        src_rows = lax.dynamic_slice_in_dim(keyval, src_tile * tile_rows, tile_rows, 0)
        keys = src_rows[:, :width].reshape(tile_rows, heads, head_dim)
        values = src_rows[:, width:].reshape(tile_rows, heads, head_dim)
        key_rel = jnp.einsum(
            "shd,hde->she", keys, w_att[rtype], preferred_element_type=jnp.float32
        ).astype(jnp.bfloat16)
        message = jnp.einsum(
            "shd,hde->she", values, w_msg[rtype], preferred_element_type=jnp.float32
        ).astype(jnp.bfloat16)
        start = dst_tile * tile_rows
        tile_q = lax.dynamic_slice_in_dim(all_queries, start, tile_rows, 0).reshape(
            tile_rows, heads, head_dim
        )
        scores = jnp.einsum("thd,shd->hts", tile_q, key_rel, preferred_element_type=jnp.float32)
        scores = scores * (relation_prior[rtype] / scale_root)[:, None, None]
        old_top = lax.dynamic_slice_in_dim(highest, start, tile_rows, 0)
        new_top = jnp.maximum(old_top, scores.max(axis=2).T)
        factor = jnp.exp(old_top - new_top)
        weight = jnp.exp(scores - new_top.T[:, :, None])
        summed = jnp.einsum(
            "hts,she->the", weight.astype(jnp.bfloat16), message, preferred_element_type=jnp.float32
        ).reshape(tile_rows, width)
        old_d = lax.dynamic_slice_in_dim(denom, start, tile_rows, 0)
        old_t = lax.dynamic_slice_in_dim(total, start, tile_rows, 0)
        highest = lax.dynamic_update_slice_in_dim(highest, new_top, start, 0)
        denom = lax.dynamic_update_slice_in_dim(
            denom, old_d * factor + weight.sum(axis=2).T, start, 0
        )
        total = lax.dynamic_update_slice_in_dim(
            total, old_t * jnp.repeat(factor, head_dim, axis=1) + summed, start, 0
        )
        return (highest, denom, total)

    init = (
        jnp.full((group_hubs, heads), -1e30, jnp.float32),
        jnp.zeros((group_hubs, heads), jnp.float32),
        jnp.zeros((group_hubs, width), jnp.float32),
    )
    highest, denom, total = lax.fori_loop(0, block_count[0], one_block, init)
    overall = lax.pmax(highest.astype(jnp.bfloat16), "dev").astype(highest.dtype)
    factor = jnp.exp(highest - overall)
    own_total, own_denom = (
        lax.psum_scatter(
            (total * jnp.repeat(factor, head_dim, axis=1)).astype(jnp.bfloat16),
            "dev",
            scatter_dimension=0,
            tiled=True,
        ).astype(jnp.float32),
        lax.psum_scatter(
            (denom * factor).astype(jnp.bfloat16), "dev", scatter_dimension=0, tiled=True
        ).astype(jnp.float32),
    )
    aggregate = (own_total / jnp.repeat(own_denom, head_dim, axis=1)).astype(jnp.bfloat16)
    return jnp.dot(aggregate, w_out, preferred_element_type=jnp.float32).astype(jnp.bfloat16)


def solution(mesh):
    placed = (
        P(("grp", "dev"), None),
        P(("grp", "dev"), None),
        P(),
        P(),
        P(),
        P(),
        P(),
        P(),
        P(),
        P(("grp", "dev"), None),
        P(("grp", "dev"), None),
        P(("grp", "dev"), None),
        P(("grp", "dev")),
    )
    return jax.shard_map(
        body, mesh=mesh, in_specs=placed, out_specs=P(("grp", "dev"), None), check_vma=False
    )
```

profile of v0, /device:TPU:0, one launch (start us, length us, event | category | flops | bytes accessed | tf_op | source)
XLA Modules:
  0.0 891.4 jit_solution(7226197442229210296)
XLA Ops:
  10.3 4.4 fusion.30
  14.7 15.1 %all-gather.3.cloned.1.call-done = bf16[512,1024]{1,0:T(8,128)(2,1)} async-done(((bf16[128,1024]{1,0:T(8,128)(2,1)}), bf16[512,1024]{1,0:T(8,128)(2,1)}) %all-gather.3.cloned.1.call-update) | async-done | bytes 1048592 | tf_op jit(solution)/shard_map/all_gather | solution.py:29
  29.8 77.1 %all-gather.5.cloned.1.call-done = bf16[1024,2048]{0,1:T(8,128)(2,1)} async-done(((bf16[128,2048]{0,1:T(8,128)(2,1)}), bf16[1024,2048]{0,1:T(8,128)(2,1)}) %all-gather.5.cloned.1.call-update) | async-done | bytes 4194320 | tf_op jit(solution)/shard_map/all_gather | solution.py:32
  108.5 501.4 %while.14 = (s32[]{:T(128)}, f32[512,16]{0,1:T(8,128)S(1)}, f32[512,16]{0,1:T(8,128)S(1)}, f32[512,1024]{0,1:T(8,128)}, s32[]{:T(128)}, /*index=5*/s32[1,40]{1,0...) while((s32[]{:T(128)}, f32[512,16]{0,1:T(8,128)S(1)}, ...), condition=%wide.region_3.0_spmd, body=%wide.region_0.0_spmd.sunk | while | flops 102766624 | bytes 8774229 | solution.py:78
  122.1 2.2 fusion.77
  124.3 2.1 constant_dynamic-update-slice_fusion.3
  140.0 2.2 fusion.77
  142.2 2.1 constant_dynamic-update-slice_fusion.3
  157.8 2.2 fusion.77
  160.0 2.1 constant_dynamic-update-slice_fusion.3
  175.7 2.2 fusion.77
  177.9 2.1 constant_dynamic-update-slice_fusion.3
  193.6 2.2 fusion.77
  195.8 2.1 constant_dynamic-update-slice_fusion.3
  211.5 2.2 fusion.77
  213.7 2.1 constant_dynamic-update-slice_fusion.3
  229.4 2.2 fusion.77
  231.6 2.1 constant_dynamic-update-slice_fusion.3
  247.2 2.2 fusion.77
  249.4 2.1 constant_dynamic-update-slice_fusion.3
  265.1 2.2 fusion.77
  267.3 2.1 constant_dynamic-update-slice_fusion.3
  283.0 2.2 fusion.77
  285.2 2.1 constant_dynamic-update-slice_fusion.3
  300.9 2.2 fusion.77
  303.1 2.1 constant_dynamic-update-slice_fusion.3
  318.8 2.2 fusion.77
  321.0 2.1 constant_dynamic-update-slice_fusion.3
  336.7 2.2 fusion.77
  338.9 2.1 constant_dynamic-update-slice_fusion.3
  354.6 2.2 fusion.77
  356.8 2.1 constant_dynamic-update-slice_fusion.3
  372.5 2.2 fusion.77
  374.7 2.1 constant_dynamic-update-slice_fusion.3
  390.4 2.2 fusion.77
  392.6 2.1 constant_dynamic-update-slice_fusion.3
  408.2 2.2 fusion.77
  410.4 2.1 constant_dynamic-update-slice_fusion.3
  426.1 2.2 fusion.77
  428.3 2.1 constant_dynamic-update-slice_fusion.3
  444.0 2.2 fusion.77
  446.2 2.1 constant_dynamic-update-slice_fusion.3
  461.9 2.2 fusion.77
  464.1 2.1 constant_dynamic-update-slice_fusion.3
  479.8 2.2 fusion.77
  482.0 2.1 constant_dynamic-update-slice_fusion.3
  497.7 2.2 fusion.77
  499.9 2.1 constant_dynamic-update-slice_fusion.3
  515.6 2.2 fusion.77
  517.8 2.1 constant_dynamic-update-slice_fusion.3
  533.5 2.2 fusion.77
  535.7 2.1 constant_dynamic-update-slice_fusion.3
  551.3 2.2 fusion.77
  553.5 2.1 constant_dynamic-update-slice_fusion.3
  569.2 2.2 fusion.77
  571.4 2.1 constant_dynamic-update-slice_fusion.3
  587.1 2.2 fusion.77
  589.3 2.1 constant_dynamic-update-slice_fusion.3
  605.0 2.2 fusion.77
  607.2 2.1 constant_dynamic-update-slice_fusion.3
  610.0 10.1 %pmax.7 = bf16[512,16]{0,1:T(8,128)(2,1)S(1)} all-reduce(bf16[512,16]{0,1:T(8,128)(2,1)S(1)} %convert_element_type.51), channel_id=1, replica_groups=mesh['grp'=8,'dev'=4] {'dev'}, use_global_device_ids=true, to_apply=%region_4.0 | all-reduce | flops 8192 | bytes 32768 | tf_op jit(solution)/shard_map/pmax | solution.py:79
  624.2 229.2 %reduce-scatter.9.cloned.1.call-done = bf16[128,16]{1,0:T(8,128)(2,1)} async-done(((bf16[512,16]{1,0:T(8,128)(2,1)}), bf16[128,16]{1,0:T(8,128)(2,1)}) %reduce-scatter.9.cloned.1.call-update) | async-done | bytes 4112
  854.2 26.7 %reduce-scatter.7.cloned.1.call-done = bf16[128,1024]{1,0:T(8,128)(2,1)} async-done(((bf16[512,1024]{1,0:T(8,128)(2,1)}), bf16[128,1024]{1,0:T(8,128)(2,1)}) %reduce-scatter.7.cloned.1.call-update) | async-done | bytes 262160
  882.1 2.8 convolution_convert_fusion.2
  (311 shorter events, 216.3 us)
Async XLA Ops:
  6.5 1.6 copy-start
  6.5 3.8 copy-start.3
  6.5 23.3 %all-gather.3.cloned.1.call-start = ((), (), s32[]{:S(2)}) async-start(), calls=%async_computation.2 | async-start | bytes 1310720 | tf_op jit(solution)/shard_map/all_gather | solution.py:29
  10.3 96.7 %all-gather.5.cloned.1.call-start = ((), (), s32[]{:S(2)}) async-start(), calls=%async_computation.3 | async-start | bytes 4718592 | tf_op jit(solution)/shard_map/all_gather | solution.py:32
  14.7 93.9 %copy-start.1 = (s32[1,40]{1,0:T(1,128)S(1)}, s32[1,40]{1,0:T(1,128)}, u32[]{:S(2)}) copy-start(s32[1,40]{1,0:T(1,128)} %param.25) | copy-start | bytes 484
  14.7 93.9 %copy-start.2 = (s32[1,40]{1,0:T(1,128)S(1)}, s32[1,40]{1,0:T(1,128)}, u32[]{:S(2)}) copy-start(s32[1,40]{1,0:T(1,128)} %param.26) | copy-start | bytes 484
  14.7 93.9 %copy-start.4 = (s32[1,40]{1,0:T(1,128)S(1)}, s32[1,40]{1,0:T(1,128)}, u32[]{:S(2)}) copy-start(s32[1,40]{1,0:T(1,128)} %param.24) | copy-start | bytes 484
  14.7 838.7 %reduce-scatter.9.cloned.1.call-start = ((), (), s32[]{:S(2)}) async-start(), calls=%async_computation.5 | async-start | bytes 163840
  620.9 259.9 %reduce-scatter.7.cloned.1.call-start = ((), (), s32[]{:S(2)}) async-start(), calls=%async_computation.4 | async-start | bytes 1310720
Sparse Core Ops, SparseCore 0:
  10.4 19.4 all-gather.2
  31.9 75.0 all-gather.4
  621.0 232.2 reduce-scatter.8
  855.9 24.8 reduce-scatter.6
where the time goes:
time: 902 us; the launch traced here: 891 us
  waiting for transfers between devices  348 us (39%)
  loops' own time  176 us (20%)
  other arithmetic  119 us (13%)
  matrix products  117 us (13%)
  local copies, waits for them, and re-layouts  107 us (12%)
  between operations  13.2 us (1%)
  blocking collectives  10.1 us (1%)
    unnamed x6, waiting for transfers between devices  256 us
    another operation x1, loops' own time, body(): highest, denom, total = lax.fori_loop(0, block_count[0], one_block, init)  176 us
    all_gather x1, waiting for transfers between devices, body(): keyval = lax.all_gather(own_kv, 'grp', axis=0, tiled=True)  77.1 us
    dot_general x28, matrix products, one_block(): jnp.einsum('hts,she->the', weight.astype(jnp.bfloat16), message, preferre...  61.1 us
    dynamic_update_slice x28, other arithmetic, one_block(): lax.dynamic_update_slice_in_dim(total, old_t * jnp.repeat(factor, head_di...  59.6 us
    dynamic_slice x56, local copies, waits for them, and re-layouts, one_block(): lax.dynamic_slice_in_dim(all_queries, start, tile_rows, 0)  50.6 us
    slice x28, local copies, waits for them, and re-layouts, one_block(): values = src_rows[:, width:].reshape(tile_rows, heads, head_dim)  49.5 us
    dot_general x28, matrix products, one_block(): jnp.einsum('thd,shd->hts', tile_q, key_rel, preferred_element_type=jnp.fl...  46.9 us
  transfers between devices with their start and end apart: 4, of which 4 were waited for; matrix products, arithmetic and copies ran while one was open for 1% of the time, Pallas kernels for 0%

commit v1 on v0

--- a/solution.py
+++ b/solution.py
@@ -2,6 +2,12 @@
 import jax.numpy as jnp
 from jax import lax
 from jax.sharding import PartitionSpec as P
+
+
+def joined_along(pieces, dim):
+    dims = list(pieces.shape[1:])
+    dims[dim] *= pieces.shape[0]
+    return jnp.moveaxis(pieces, 0, dim).reshape(dims)
 
 
 def body(
@@ -29,7 +35,19 @@
     all_queries = lax.all_gather(queries, "dev", axis=0, tiled=True)
     w_both = jnp.concatenate([w_key, w_value], axis=1)
     own_kv = jnp.dot(node_src, w_both, preferred_element_type=jnp.float32).astype(jnp.bfloat16)
-    keyval = lax.all_gather(own_kv, "grp", axis=0, tiled=True)
+    size = lax.axis_size("grp")
+    pairs = [(i, (i + 1) % size) for i in range(size)]
+    back = [(b, a) for a, b in pairs]
+    lower, upper = ([], [])
+    for lap in range(size - 1):
+        if lap % 2 == 0:
+            lower.append(lax.ppermute(lower[-1] if lower else own_kv, "grp", pairs))
+        else:
+            upper.append(lax.ppermute(upper[-1] if upper else own_kv, "grp", back))
+    parts = jnp.stack([*lower[::-1], own_kv, *upper])
+    shift = lax.axis_index("grp") - len(lower)
+    parts = parts[(jnp.arange(size) - shift) % size]
+    keyval = joined_along(parts, 0)
     scale_root = jnp.sqrt(jnp.float32(head_dim))
 
     def one_block(slot, carry):

time: 902 us -> 982 us (1.089)
  local copies, waits for them, and re-layouts: 107 us -> 166 us
  starting transfers between devices: 0.13 us -> 37.6 us
  waiting for transfers between devices: 348 us -> 320 us
  loops' own time: 176 us -> 188 us
    all_gather x1 -> x0, waiting for transfers between devices: 77.1 us -> none  [body(): keyval = lax.all_gather(own_kv, 'grp', axis=0, tiled=True)]
    while x0 -> x56, local copies, waits for them, and re-layouts: none -> 54.7 us
    ppermute x0 -> x7, waiting for transfers between devices: none -> 48.7 us  [the longest x4 48.7 us: body(): lower.append(lax.ppermute(lower[-1] if lower else own_kv, 'grp', pairs))]
    ppermute x0 -> x7, starting transfers between devices: none -> 37.5 us  [the longest x3 29.4 us: body(): upper.append(lax.ppermute(upper[-1] if upper else own_kv, 'grp', back))]
    dynamic_slice x56, local copies, waits for them, and re-layouts: 50.6 us -> 32 us  [one_block(): lax.dynamic_slice_in_dim(all_queries, start, tile_rows, 0)]
    unnamed x6 -> x5, waiting for transfers between devices: 256 us -> 272 us
    all_gather x1, waiting for transfers between devices: 15.1 us -> 0.01 us  [body(): all_queries = lax.all_gather(queries, 'dev', axis=0, tiled=True)]
    another operation x1, loops' own time: 176 us -> 188 us  [body(): highest, denom, total = lax.fori_loop(0, block_count[0], one_block, init)]
  transfers between devices with their start and end apart: 4 -> 10, of which waited for: 4 -> 6; matrix products, arithmetic and copies ran while one was open for 1% -> 3% of each run, Pallas kernels for 0% -> 0%
where the time goes in v1:
time: 982 us; the launch traced here: 970 us
  waiting for transfers between devices  320 us (33%)
  loops' own time  188 us (19%)
  local copies, waits for them, and re-layouts  166 us (17%)
  other arithmetic  122 us (12%)
  matrix products  114 us (12%)
  starting transfers between devices  37.6 us (4%)
  between operations  13.2 us (1%)
  blocking collectives  10.1 us (1%)
    unnamed x5, waiting for transfers between devices  272 us
    another operation x1, loops' own time, body(): highest, denom, total = lax.fori_loop(0, block_count[0], one_block, init)  188 us
    dot_general x28, matrix products, one_block(): jnp.einsum('hts,she->the', weight.astype(jnp.bfloat16), message, preferre...  61.5 us
    dynamic_update_slice x28, other arithmetic, one_block(): lax.dynamic_update_slice_in_dim(total, old_t * jnp.repeat(factor, head_di...  59.9 us
    while x56, local copies, waits for them, and re-layouts  54.7 us
    slice x28, local copies, waits for them, and re-layouts, one_block(): values = src_rows[:, width:].reshape(tile_rows, heads, head_dim)  49.6 us
    ppermute x4, waiting for transfers between devices, body(): lower.append(lax.ppermute(lower[-1] if lower else own_kv, 'grp', pairs))  48.7 us
    dot_general x28, matrix products, one_block(): jnp.einsum('thd,shd->hts', tile_q, key_rel, preferred_element_type=jnp.fl...  44.7 us
  transfers between devices with their start and end apart: 10, of which 6 were waited for; matrix products, arithmetic and copies ran while one was open for 3% of the time, Pallas kernels for 0%

profile of v1, /device:TPU:0, one launch (start us, length us, event | category | flops | bytes accessed | tf_op | source)
XLA Modules:
  0.0 970.2 jit_solution(3539189784006678236)
XLA Ops:
  6.5 3.7 fusion.27
  10.2 3.0 collective-permute-start
  13.2 15.0 %collective-permute-done = bf16[128,2048]{0,1:T(8,128)(2,1)S(1)} collective-permute-done((bf16[128,2048]{0,1:T(8,128)(2,1)S(1)}, bf16[128,2048]{0,1:T(8,128)(2,1)S(1)}, u32[]{:S(2)}, u32[]{:S(2)}) %collective-permute-start) | collective-permute-done | bytes 524320 | tf_op jit(solution)/shard_map/ppermute | solution.py:44
  28.2 4.7 collective-permute-start.4
  32.9 17.4 %collective-permute-done.1 = bf16[128,2048]{0,1:T(8,128)(2,1)S(1)} collective-permute-done((bf16[128,2048]{0,1:T(8,128)(2,1)S(1)}, bf16[128,2048]{0,1:T(8,128)(2,1)S(1)}, u32[]{:S(2)}, u32[]{:S(2)}) %collective-permute-start.1) | collective-permute-done | bytes 524320 | tf_op jit(solution)/shard_map/ppermute | solution.py:44
  50.3 2.5 collective-permute-start.2
  52.8 12.2 %collective-permute-start.5 = (bf16[128,2048]{0,1:T(8,128)(2,1)}, bf16[128,2048]{0,1:T(8,128)(2,1)}, u32[]{:S(2)}, u32[]{:S(2)}) collective-permute-start(bf16[128,2048]{0,1:T(8,128)(2,1)} %collective-permute-done.4), channel_id=1, source_target_pairs={{4,0},{8,4},{12,8},{16,12},{20,16},{24,20},{28,24},{0,28},{5,1},{9... | collective-permute-start | bytes 1572872 | tf_op jit(solution)/shard_map/ppermute | solution.py:46
  65.0 9.1 collective-permute-done.2
  74.2 2.6 collective-permute-start.3
  78.0 12.5 %collective-permute-start.6 = (bf16[128,2048]{0,1:T(8,128)(2,1)}, bf16[128,2048]{0,1:T(8,128)(2,1)S(1)}, u32[]{:S(2)}, u32[]{:S(2)}) collective-permute-start(bf16[128,2048]{0,1:T(8,128)(2,1)} %collective-permute-done.5), channel_id=1, source_target_pairs={{4,0},{8,4},{12,8},{16,12},{20,16},{24,20},{28,24},{0,28},{5,1},{9... | collective-permute-start | bytes 1572872 | tf_op jit(solution)/shard_map/ppermute | solution.py:46
  90.5 7.1 collective-permute-done.3
  109.6 5.2 gather_fusion
  114.8 6.5 copy.21
  123.0 550.2 %while.14 = (s32[]{:T(128)}, f32[512,16]{0,1:T(8,128)S(1)}, f32[512,16]{0,1:T(8,128)S(1)}, f32[512,1024]{0,1:T(8,128)}, s32[]{:T(128)}, /*index=5*/s32[1,40]{1,0...) while((s32[]{:T(128)}, f32[512,16]{0,1:T(8,128)S(1)}, ...), condition=%wide.region_3.4_spmd, body=%wide.region_0.3_spmd.sunk | while | flops 102766624 | bytes 9822797 | solution.py:96
  138.1 2.2 fusion.76
  157.7 2.2 fusion.76
  177.3 2.2 fusion.76
  179.7 2.1 constant_dynamic-update-slice_fusion.3
  196.9 2.2 fusion.76
  199.3 2.2 constant_dynamic-update-slice_fusion.3
  216.6 2.2 fusion.76
  236.2 2.2 fusion.76
  238.6 2.1 constant_dynamic-update-slice_fusion.3
  255.8 2.2 fusion.76
  258.2 2.2 constant_dynamic-update-slice_fusion.3
  275.4 2.2 fusion.76
  277.8 2.2 constant_dynamic-update-slice_fusion.3
  295.1 2.2 fusion.76
  297.5 2.2 constant_dynamic-update-slice_fusion.3
  314.7 2.2 fusion.76
  317.1 2.1 constant_dynamic-update-slice_fusion.3
  334.3 2.2 fusion.76
  336.7 2.2 constant_dynamic-update-slice_fusion.3
  354.0 2.2 fusion.76
  356.4 2.2 constant_dynamic-update-slice_fusion.3
  373.6 2.2 fusion.76
  393.2 2.2 fusion.76
  395.6 2.2 constant_dynamic-update-slice_fusion.3
  412.9 2.2 fusion.76
  432.5 2.2 fusion.76
  434.9 2.1 constant_dynamic-update-slice_fusion.3
  452.1 2.2 fusion.76
  471.7 2.2 fusion.76
  474.1 2.2 constant_dynamic-update-slice_fusion.3
  491.4 2.2 fusion.76
  493.7 2.2 constant_dynamic-update-slice_fusion.3
  511.0 2.2 fusion.76
  513.4 2.2 constant_dynamic-update-slice_fusion.3
  530.6 2.2 fusion.76
  533.0 2.1 constant_dynamic-update-slice_fusion.3
  550.2 2.2 fusion.76
  552.6 2.2 constant_dynamic-update-slice_fusion.3
  569.9 2.2 fusion.76
  589.5 2.2 fusion.76
  609.1 2.2 fusion.76
  628.7 2.2 fusion.76
  648.3 2.2 fusion.76
  650.7 2.2 constant_dynamic-update-slice_fusion.3
  668.0 2.2 fusion.76
  670.4 2.2 constant_dynamic-update-slice_fusion.3
  673.2 10.1 %pmax.7 = bf16[512,16]{0,1:T(8,128)(2,1)S(1)} all-reduce(bf16[512,16]{0,1:T(8,128)(2,1)S(1)} %convert_element_type.51), channel_id=1, replica_groups=mesh['grp'=8,'dev'=4] {'dev'}, use_global_device_ids=true, to_apply=%region_4.5 | all-reduce | flops 8192 | bytes 32768 | tf_op jit(solution)/shard_map/pmax | solution.py:97
  687.4 244.7 %reduce-scatter.9.cloned.1.call-done = bf16[128,16]{1,0:T(8,128)(2,1)} async-done(((bf16[512,16]{1,0:T(8,128)(2,1)}), bf16[128,16]{1,0:T(8,128)(2,1)}) %reduce-scatter.9.cloned.1.call-update) | async-done | bytes 4112
  932.9 26.8 %reduce-scatter.7.cloned.1.call-done = bf16[128,1024]{1,0:T(8,128)(2,1)} async-done(((bf16[512,1024]{1,0:T(8,128)(2,1)}), bf16[128,1024]{1,0:T(8,128)(2,1)}) %reduce-scatter.7.cloned.1.call-update) | async-done | bytes 262160
  960.9 2.8 convolution_convert_fusion.2
  (392 shorter events, 283.0 us)
Async XLA Ops:
  6.5 70.2 %copy-start = (bf16[1024,1024]{1,0:T(8,128)(2,1)S(1)}, bf16[1024,1024]{1,0:T(8,128)(2,1)}, u32[]{:S(2)}) copy-start(bf16[1024,1024]{1,0:T(8,128)(2,1)} %param.17) | copy-start | bytes 6291460
  6.5 70.2 %copy-start.2 = (bf16[128,1024]{1,0:T(8,128)(2,1)S(1)}, bf16[128,1024]{1,0:T(8,128)(2,1)}, u32[]{:S(2)}) copy-start(bf16[128,1024]{1,0:T(8,128)(2,1)} %param.16) | copy-start | bytes 786436
  6.5 114.8 %all-gather.2.cloned.1.call-start = ((), (), s32[]{:S(2)}) async-start(), calls=%async_computation.2 | async-start | bytes 1310720 | tf_op jit(solution)/shard_map/all_gather | solution.py:35
  10.2 18.0 %collective-permute-start = (bf16[128,2048]{0,1:T(8,128)(2,1)S(1)}, bf16[128,2048]{0,1:T(8,128)(2,1)S(1)}, u32[]{:S(2)}, u32[]{:S(2)}) collective-permute-start(bf16[128,2048]{0,1:T(8,128)(2,1)S(1)} %bitcast.131), channel_id=1, source_target_pairs={{0,4},{4,8},{8,12},{12,16},{16,20},{20,24},{24,28},{28,0},{1,5},{5... | collective-permute-start | bytes 1572872 | tf_op jit(solution)/shard_map/ppermute | solution.py:44
  28.2 22.1 %collective-permute-start.1 = (bf16[128,2048]{0,1:T(8,128)(2,1)S(1)}, bf16[128,2048]{0,1:T(8,128)(2,1)S(1)}, u32[]{:S(2)}, u32[]{:S(2)}) collective-permute-start(bf16[128,2048]{0,1:T(8,128)(2,1)S(1)} %collective-permute-done), channel_id=1, source_target_pairs={{0,4},{4,8},{8,12},{12,16},{16,20},{20,24},{24,28},{28,0},{1,5},{5... | collective-permute-start | bytes 1572872 | tf_op jit(solution)/shard_map/ppermute | solution.py:44
  28.2 24.6 %collective-permute-start.4 = (bf16[128,2048]{0,1:T(8,128)(2,1)S(1)}, bf16[128,2048]{0,1:T(8,128)(2,1)}, u32[]{:S(2)}, u32[]{:S(2)}) collective-permute-start(bf16[128,2048]{0,1:T(8,128)(2,1)S(1)} %bitcast.132), channel_id=1, source_target_pairs={{4,0},{8,4},{12,8},{16,12},{20,16},{24,20},{28,24},{0,28},{5,1},{9... | collective-permute-start | bytes 1572872 | tf_op jit(solution)/shard_map/ppermute | solution.py:46
  50.3 2.5 copy-start.1
  50.3 23.9 %collective-permute-start.2 = (bf16[128,2048]{0,1:T(8,128)(2,1)S(1)}, bf16[128,2048]{0,1:T(8,128)(2,1)}, u32[]{:S(2)}, u32[]{:S(2)}) collective-permute-start(bf16[128,2048]{0,1:T(8,128)(2,1)S(1)} %collective-permute-done.1), channel_id=1, source_target_pairs={{0,4},{4,8},{8,12},{12,16},{16,20},{20,24},{24,28},{28,0},{1,5},{5... | collective-permute-start | bytes 1572872 | tf_op jit(solution)/shard_map/ppermute | solution.py:44
  52.8 25.2 %collective-permute-start.5 = (bf16[128,2048]{0,1:T(8,128)(2,1)}, bf16[128,2048]{0,1:T(8,128)(2,1)}, u32[]{:S(2)}, u32[]{:S(2)}) collective-permute-start(bf16[128,2048]{0,1:T(8,128)(2,1)} %collective-permute-done.4), channel_id=1, source_target_pairs={{4,0},{8,4},{12,8},{16,12},{20,16},{24,20},{28,24},{0,28},{5,1},{9... | collective-permute-start | bytes 1572872 | tf_op jit(solution)/shard_map/ppermute | solution.py:46
  74.2 23.5 %collective-permute-start.3 = (bf16[128,2048]{0,1:T(8,128)(2,1)}, bf16[128,2048]{0,1:T(8,128)(2,1)}, u32[]{:S(2)}, u32[]{:S(2)}) collective-permute-start(bf16[128,2048]{0,1:T(8,128)(2,1)} %collective-permute-done.2), channel_id=1, source_target_pairs={{0,4},{4,8},{8,12},{12,16},{16,20},{20,24},{24,28},{28,0},{1,5},{5... | collective-permute-start | bytes 1572872 | tf_op jit(solution)/shard_map/ppermute | solution.py:44
  78.0 854.1 %reduce-scatter.9.cloned.1.call-start = ((), (), s32[]{:S(2)}) async-start(), calls=%async_computation.4 | async-start | bytes 163840
  78.0 30.7 %collective-permute-start.6 = (bf16[128,2048]{0,1:T(8,128)(2,1)}, bf16[128,2048]{0,1:T(8,128)(2,1)S(1)}, u32[]{:S(2)}, u32[]{:S(2)}) collective-permute-start(bf16[128,2048]{0,1:T(8,128)(2,1)} %collective-permute-done.5), channel_id=1, source_target_pairs={{4,0},{8,4},{12,8},{16,12},{20,16},{24,20},{28,24},{0,28},{5,1},{9... | collective-permute-start | bytes 1572872 | tf_op jit(solution)/shard_map/ppermute | solution.py:46
  114.8 8.1 copy-start.3
  114.8 8.2 copy-start.4
  114.8 8.2 copy-start.5
  684.1 275.6 %reduce-scatter.7.cloned.1.call-start = ((), (), s32[]{:S(2)}) async-start(), calls=%async_computation.3 | async-start | bytes 1310720
Sparse Core Ops, SparseCore 0:
  78.1 15.1 all-gather.1
  684.3 247.8 reduce-scatter.8
  934.8 24.8 reduce-scatter.6
